TPU v7x, 256 devices: a whole 4x4x8 slice. The times are simulated.
256 devices in a mesh: seq: 32 (over z, y), head: 8 (over x, core).
Axes of the slice: x: 4, y: 4, z: 8, core: 2. Of those that a mesh axis runs over, the one named last changes fastest.
Arguments:
- query_in: bfloat16 [32768, 32, 128], P(('seq', 'head')), may hold values from -6 to 6
- key_in: bfloat16 [32768, 32, 128], P(('seq', 'head')), may hold values from -6 to 6
- value_in: bfloat16 [32768, 32, 128], P(('seq', 'head')), may hold values from -6 to 6
- grad_out: bfloat16 [32768, 32, 128], P(('seq', 'head')), may hold values from -6 to 6
- log_decay: bfloat16 [32768, 32], P(('seq', 'head')), may hold values from -1 to 0, as said below
Outputs:
- attended: bfloat16 [32768, 32, 128], P(('seq', 'head'))
- grad_query: bfloat16 [32768, 32, 128], P(('seq', 'head'))
- grad_key: bfloat16 [32768, 32, 128], P(('seq', 'head'))
- grad_value: bfloat16 [32768, 32, 128], P(('seq', 'head'))
Inputs may be any that keep to these rules, and one draw needn't show every extreme that they name: Every entry of log_decay is negative.
All inputs are finite; a program needn't handle non-finite values.
Results may differ from a plain program's by a relative error of at most 0.007.
Values may be sent and summed in bfloat16 or wider, within the bound.
A program may use at most 128 MiB of HBM per device.

v0:
```python
import jax
import jax.numpy as jnp
from jax import lax
from jax.sharding import PartitionSpec as P

precise = lax.Precision.HIGHEST


def shards(query_in, key_in, value_in, grad_out, log_decay):
    f32 = jnp.float32
    bf16 = jnp.bfloat16
    queries, keys_all, values, grads, token_decays = (
        lax.all_to_all(query_in, "head", split_axis=1, concat_axis=0, tiled=True),
        lax.all_to_all(key_in, "head", split_axis=1, concat_axis=0, tiled=True),
        lax.all_to_all(value_in, "head", split_axis=1, concat_axis=0, tiled=True),
        lax.all_to_all(grad_out, "head", split_axis=1, concat_axis=0, tiled=True),
        lax.all_to_all(log_decay, "head", split_axis=1, concat_axis=0, tiled=True),
    )
    segment_length = queries.shape[0]
    width = queries.shape[2]
    scaling = 1.0 / width
    within = jnp.cumsum(token_decays.astype(f32), axis=0)
    seg_total = within[-1]
    to_start = jnp.exp(within)[:, :, None]
    to_end = jnp.exp(seg_total[None, :] - within)[:, :, None]
    keys_end = (keys_all.astype(f32) * to_end).astype(bf16)
    values_end = (values.astype(f32) * to_end).astype(bf16)
    queries_start = (queries.astype(f32) * to_start).astype(bf16)
    grads_start = (grads.astype(f32) * to_start).astype(bf16)
    local_kv = jnp.einsum("thd,the->hde", keys_end, values, preferred_element_type=f32).astype(bf16)
    local_qg = jnp.einsum("thd,the->hde", queries_start, grads, preferred_element_type=f32).astype(
        bf16
    )
    seg_count = lax.axis_size("seq")
    seq_place = lax.axis_index("seq")
    totals = lax.all_gather(seg_total[None, :], "seq", axis=0, tiled=True)
    cum_inc = jnp.cumsum(totals, axis=0)
    cum_exc = cum_inc - totals
    mine_inc = lax.dynamic_index_in_dim(cum_inc, seq_place, 0, keepdims=False)
    mine_exc = lax.dynamic_index_in_dim(cum_exc, seq_place, 0, keepdims=False)
    ranks = jnp.arange(seg_count)[:, None]
    earlier = ranks < seq_place
    later_on = ranks > seq_place
    w_in = jnp.where(earlier, jnp.exp(jnp.where(earlier, mine_exc[None, :] - cum_inc, 0.0)), 0.0)
    w_out = jnp.where(later_on, jnp.exp(jnp.where(later_on, cum_exc - mine_inc[None, :], 0.0)), 0.0)
    new_in = jnp.einsum(
        "ih,ihde->hde",
        w_in,
        lax.all_gather(local_kv[None], "seq", axis=0, tiled=True).astype(f32),
        precision=precise,
    )
    new_out = jnp.einsum(
        "ih,ihde->hde",
        w_out,
        lax.all_gather(local_qg[None], "seq", axis=0, tiled=True).astype(f32),
        precision=precise,
    )
    state_in = new_in
    state_out = new_out
    state_in = state_in.astype(bf16)
    state_out = state_out.astype(bf16)
    head_specific = within.T
    causal = jnp.arange(segment_length)[:, None] >= jnp.arange(segment_length)[None, :]
    decay_mat = jnp.where(
        causal,
        jnp.exp(jnp.where(causal, head_specific[:, :, None] - head_specific[:, None, :], 0.0)),
        0.0,
    )
    scores = jnp.einsum("thd,shd->hts", queries, keys_all, preferred_element_type=f32)
    attn_w = (scaling * scores * decay_mat).astype(bf16)
    intra = jnp.einsum("hts,shd->thd", attn_w, values, preferred_element_type=f32)
    attended = (
        intra
        + scaling * jnp.einsum("thd,hde->the", queries_start, state_in, preferred_element_type=f32)
    ).astype(bf16)
    back_raw = jnp.einsum("the,she->hts", grads, values, preferred_element_type=f32)
    back_w = (scaling * back_raw * decay_mat).astype(bf16)
    grad_query = (
        jnp.einsum("hts,shd->thd", back_w, keys_all, preferred_element_type=f32)
        + scaling * jnp.einsum("the,hde->thd", grads_start, state_in, preferred_element_type=f32)
    ).astype(bf16)
    grad_key = (
        jnp.einsum("hts,thd->shd", back_w, queries, preferred_element_type=f32)
        + scaling * jnp.einsum("she,hde->shd", values_end, state_out, preferred_element_type=f32)
    ).astype(bf16)
    grad_value = (
        jnp.einsum("hts,the->she", attn_w, grads, preferred_element_type=f32)
        + scaling * jnp.einsum("shd,hde->she", keys_end, state_out, preferred_element_type=f32)
    ).astype(bf16)
    results = (
        lax.all_to_all(attended, "head", split_axis=0, concat_axis=1, tiled=True),
        lax.all_to_all(grad_query, "head", split_axis=0, concat_axis=1, tiled=True),
        lax.all_to_all(grad_key, "head", split_axis=0, concat_axis=1, tiled=True),
        lax.all_to_all(grad_value, "head", split_axis=0, concat_axis=1, tiled=True),
    )
    return (results[0], results[1], results[2], results[3])


def solution(mesh):
    return jax.shard_map(
        shards,
        mesh=mesh,
        in_specs=(
            P(("seq", "head"), None, None),
            P(("seq", "head"), None, None),
            P(("seq", "head"), None, None),
            P(("seq", "head"), None, None),
            P(("seq", "head"), None),
        ),
        out_specs=(
            P(("seq", "head"), None, None),
            P(("seq", "head"), None, None),
            P(("seq", "head"), None, None),
            P(("seq", "head"), None, None),
        ),
        check_vma=False,
    )
```

profile of v0, /device:TPU:1, one launch (start us, length us, event | category | flops | bytes accessed | tf_op | source)
XLA Modules:
  0.0 301.6 jit_solution(2192634646455913351)
XLA Ops:
  7.2 6.6 %all-to-all-start.2 = ((bf16[128,8,4]{0,2,1:T(4,128)(2,1)}), bf16[128,8,4]{0,2,1:T(4,128)(2,1)S(1)}, u32[]{:S(2)}, u32[]{:S(2)}) async-start(bf16[128,8,4]{0,2,1:T(4,128)(2,1)} %bitcast.154), calls=%async_computation.2 | async-start | bytes 16384 | tf_op jit(solution)/shard_map/all_to_all | solution.py:17
  13.8 2.6 copy.120
  16.4 2.0 all-to-all-done.2
  18.4 4.2 %all-to-all-start.1 = ((bf16[128,32,128]{2,0,1:T(8,128)(2,1)}), bf16[128,32,128]{2,0,1:T(8,128)(2,1)S(1)}, u32[]{:S(2)}, u32[]{:S(2)}) async-start(bf16[128,32,128]{2,0,1:T(8,128)(2,1)} %copy.120), calls=%async_computation.1 | async-start | bytes 2097152 | tf_op jit(solution)/shard_map/all_to_all | solution.py:14
  22.6 1.4 copy.122
  24.0 13.7 %all-to-all-done.1 = bf16[128,32,128]{2,0,1:T(8,128)(2,1)S(1)} async-done(((bf16[128,32,128]{2,0,1:T(8,128)(2,1)}), bf16[128,32,128]{2,0,1:T(8,128)(2,1)S(1)}, u32[]{:S(2)}, u32[]{:S(2)}) %all-to-all-start.1) | async-done | bytes 1048608 | tf_op jit(solution)/shard_map/all_to_all | solution.py:14
  37.7 4.3 %all-to-all-start.3 = ((bf16[128,32,128]{2,0,1:T(8,128)(2,1)}), bf16[128,32,128]{2,0,1:T(8,128)(2,1)S(1)}, u32[]{:S(2)}, u32[]{:S(2)}) async-start(bf16[128,32,128]{2,0,1:T(8,128)(2,1)} %copy.122), calls=%async_computation.3 | async-start | bytes 2097152 | tf_op jit(solution)/shard_map/all_to_all | solution.py:15
  42.1 1.1 reduce-window.6
  44.0 13.1 %all-to-all-done.3 = bf16[128,32,128]{2,0,1:T(8,128)(2,1)S(1)} async-done(((bf16[128,32,128]{2,0,1:T(8,128)(2,1)}), bf16[128,32,128]{2,0,1:T(8,128)(2,1)S(1)}, u32[]{:S(2)}, u32[]{:S(2)}) %all-to-all-start.3) | async-done | bytes 1048608 | tf_op jit(solution)/shard_map/all_to_all | solution.py:15
  57.3 1.0 copy-done.4
  58.2 2.0 convolution_convert_fusion.1
  60.3 2.6 copy.118
  62.9 4.3 %all-to-all-start = ((bf16[128,32,128]{2,0,1:T(8,128)(2,1)}), bf16[128,32,128]{2,0,1:T(8,128)(2,1)S(1)}, u32[]{:S(2)}, u32[]{:S(2)}) async-start(bf16[128,32,128]{2,0,1:T(8,128)(2,1)} %copy.118), calls=%async_computation | async-start | bytes 2097152 | tf_op jit(solution)/shard_map/all_to_all | solution.py:13
  67.2 1.4 copy.132
  68.6 13.7 %all-to-all-done = bf16[128,32,128]{2,0,1:T(8,128)(2,1)S(1)} async-done(((bf16[128,32,128]{2,0,1:T(8,128)(2,1)}), bf16[128,32,128]{2,0,1:T(8,128)(2,1)S(1)}, u32[]{:S(2)}, u32[]{:S(2)}) %all-to-all-start) | async-done | bytes 1048608 | tf_op jit(solution)/shard_map/all_to_all | solution.py:13
  82.3 4.3 %all-to-all-start.5 = ((bf16[128,32,128]{2,0,1:T(8,128)(2,1)}), bf16[128,32,128]{2,0,1:T(8,128)(2,1)S(1)}, u32[]{:S(2)}, u32[]{:S(2)}) async-start(bf16[128,32,128]{2,0,1:T(8,128)(2,1)} %copy.132), calls=%async_computation.5 | async-start | bytes 2097152 | tf_op jit(solution)/shard_map/all_to_all | solution.py:16
  86.8 15.0 %all-to-all-done.5 = bf16[128,32,128]{2,0,1:T(8,128)(2,1)S(1)} async-done(((bf16[128,32,128]{2,0,1:T(8,128)(2,1)}), bf16[128,32,128]{2,0,1:T(8,128)(2,1)S(1)}, u32[]{:S(2)}, u32[]{:S(2)}) %all-to-all-start.5) | async-done | bytes 1048608 | tf_op jit(solution)/shard_map/all_to_all | solution.py:16
  101.9 2.0 convolution_convert_fusion
  104.2 37.7 %all-gather.2 = f32[32,1,4]{2,1,0:T(1,128)S(1)} all-gather(f32[1,1,4]{2,1,0:T(1,128)S(1)} %bitcast.155), channel_id=1, replica_groups=mesh['seq'=32,'head'=8] {'seq'}, dimensions={0}, use_global_device_ids=true | all-gather | bytes 528 | tf_op jit(solution)/shard_map/all_gather | solution.py:36
  142.4 7.4 %multiply_convert_fusion = bf16[4,1024,1024]{2,1,0:T(8,128)(2,1)S(1)} fusion(bf16[1024,4,128]{2,0,1:T(8,128)(2,1)S(1)} %bitcast.118, bf16[1024,4,128]{2,0,1:T(8,128)(2,1)} %bitcast.139, f32[4,1024]{1,0:T(4,128)S(1)} %bitcast.150, pred[1024,1024]{1,0:T(8,128)(4,1)S(1)} %iota_compare_fusion), kind=kOutput, calls=%fused_computation | convolution fusion | flops 1098907648 | bytes 11550720 | tf_op jit(solution)/shard_map/the,she->hts/dot_general | solution.py:76
  149.8 4.0 %fusion.14 = f32[4,1024,128]{2,1,0:T(8,128)} fusion(bf16[4,1024,1024]{2,1,0:T(8,128)(2,1)S(1)} %multiply_convert_fusion, bf16[1024,4,128]{2,0,1:T(8,128)(2,1)S(1)} %bitcast.135), kind=kOutput, calls=%fused_computation.43 | convolution fusion | flops 1073741824 | bytes 11534336 | tf_op jit(solution)/shard_map/hts,shd->thd/dot_general | solution.py:79
  153.8 7.8 %multiply_convert_fusion.1 = bf16[4,1024,1024]{2,1,0:T(8,128)(2,1)} fusion(bf16[1024,4,128]{2,0,1:T(8,128)(2,1)S(1)} %bitcast.122, bf16[1024,4,128]{2,0,1:T(8,128)(2,1)S(1)} %bitcast.136, f32[4,1024]{1,0:T(4,128)S(1)} %bitcast.151, pred[1024,1024]{1,0:T(8,128)(4,1)S(1)} %iota_compare_fusion), kind=kOutput, calls=%fused_computation.1 | convolution fusion | flops 1098907648 | bytes 11550720 | tf_op jit(solution)/shard_map/thd,shd->hts/dot_general | solution.py:69
  161.6 5.8 %fusion = f32[4,1,128,128]{3,1,2,0:T(1,128)S(1)} fusion(f32[32,4,1,1]{0,2,3,1:T(1,128)S(1)} %copy.148, bf16[32,4,128,128]{3,2,1,0:T(8,128)(2,1)} %bitcast.125), kind=kOutput, calls=%fused_computation.4 | convolution fusion | flops 25165824 | bytes 4456960 | tf_op jit(solution)/shard_map/ih,ihde->hde/dot_general | solution.py:46
  167.4 1.0 fusion.4
  168.4 1.8 copy.135
  170.2 8.2 %all-to-all-start.6 = ((bf16[1024,4,128]{2,1,0:T(4,128)(2,1)}), bf16[1024,4,128]{2,1,0:T(4,128)(2,1)S(1)}, u32[]{:S(2)}, u32[]{:S(2)}) async-start(bf16[1024,4,128]{2,1,0:T(4,128)(2,1)} %copy.135), calls=%async_computation.6 | async-start | bytes 2097152 | tf_op jit(solution)/shard_map/all_to_all | solution.py:92
  178.4 7.7 %fusion.15 = f32[4,1024,128]{2,1,0:T(8,128)} fusion(bf16[4,1024,1024]{2,1,0:T(8,128)(2,1)} %copy-done, bf16[1024,4,128]{2,0,1:T(8,128)(2,1)S(1)} %bitcast.123), kind=kOutput, calls=%fused_computation.44 | convolution fusion | flops 1073741824 | bytes 11534336 | tf_op jit(solution)/shard_map/hts,thd->shd/dot_general | solution.py:83
  186.1 36.4 %all-gather.8.cloned.1.call-done = bf16[128,128,128]{2,1,0:T(8,128)(2,1)} async-done(((bf16[4,128,128]{2,1,0:T(8,128)(2,1)}), bf16[128,128,128]{2,1,0:T(8,128)(2,1)}) %all-gather.8.cloned.1.call-update) | async-done | bytes 4194320 | tf_op jit(solution)/shard_map/all_gather | solution.py:55
  222.5 3.7 %multiply_reduce_fusion = bf16[4,128,128]{2,1,0:T(8,128)(2,1)} fusion(bf16[4,32,128,128]{3,2,0,1:T(8,128)(2,1)} %bitcast.126, f32[4,32]{0,1:T(8,128)S(1)} %get-tuple-element.4), kind=kLoop, calls=%fused_computation.3 | loop fusion | flops 6225920 | bytes 4325888
  226.3 1.0 copy.162
  227.3 2.7 fusion.3
  230.0 1.8 copy.141
  231.8 7.6 %all-to-all-start.7 = ((bf16[1024,4,128]{2,1,0:T(4,128)(2,1)}), bf16[1024,4,128]{2,1,0:T(4,128)(2,1)}, u32[]{:S(2)}, u32[]{:S(2)}) async-start(bf16[1024,4,128]{2,1,0:T(4,128)(2,1)} %copy.141), calls=%async_computation.7 | async-start | bytes 2097152 | tf_op jit(solution)/shard_map/all_to_all | solution.py:93
  239.3 5.9 %fusion.13 = f32[4,1024,128]{2,1,0:T(8,128)S(1)} fusion(bf16[4,1024,1024]{2,1,0:T(8,128)(2,1)} %multiply_convert_fusion.1, bf16[1024,4,128]{2,0,1:T(8,128)(2,1)} %bitcast.141), kind=kOutput, calls=%fused_computation.42 | convolution fusion | flops 1073741824 | bytes 11534336 | tf_op jit(solution)/shard_map/hts,shd->thd/dot_general | solution.py:71
  245.3 1.0 fusion.5
  246.3 1.8 copy.130
  248.1 6.5 %all-to-all-done.7 = bf16[1024,4,128]{2,1,0:T(4,128)(2,1)} async-done(((bf16[1024,4,128]{2,1,0:T(4,128)(2,1)}), bf16[1024,4,128]{2,1,0:T(4,128)(2,1)}, u32[]{:S(2)}, u32[]{:S(2)}) %all-to-all-start.7) | async-done | bytes 1048608 | tf_op jit(solution)/shard_map/all_to_all | solution.py:93
  254.5 4.3 %all-to-all-start.4 = ((bf16[1024,4,128]{2,1,0:T(4,128)(2,1)}), bf16[1024,4,128]{2,1,0:T(4,128)(2,1)S(1)}, u32[]{:S(2)}, u32[]{:S(2)}) async-start(bf16[1024,4,128]{2,1,0:T(4,128)(2,1)} %copy.130), calls=%async_computation.4 | async-start | bytes 2097152 | tf_op jit(solution)/shard_map/all_to_all | solution.py:91
  258.9 6.4 %fusion.16 = f32[4,1024,128]{2,1,0:T(8,128)S(1)} fusion(bf16[4,1024,1024]{2,1,0:T(8,128)(2,1)} %multiply_convert_fusion.1, bf16[1024,4,128]{2,0,1:T(8,128)(2,1)S(1)} %bitcast.120), kind=kOutput, calls=%fused_computation.45 | convolution fusion | flops 1073741824 | bytes 11534336 | tf_op jit(solution)/shard_map/hts,the->she/dot_general | solution.py:87
  265.3 1.0 fusion.2
  266.3 1.8 copy.145
  268.1 5.9 %all-to-all-done.4 = bf16[1024,4,128]{2,1,0:T(4,128)(2,1)S(1)} async-done(((bf16[1024,4,128]{2,1,0:T(4,128)(2,1)}), bf16[1024,4,128]{2,1,0:T(4,128)(2,1)S(1)}, u32[]{:S(2)}, u32[]{:S(2)}) %all-to-all-start.4) | async-done | bytes 1048608 | tf_op jit(solution)/shard_map/all_to_all | solution.py:91
  274.0 4.3 %all-to-all-start.8 = ((bf16[1024,4,128]{2,1,0:T(4,128)(2,1)}), bf16[1024,4,128]{2,1,0:T(4,128)(2,1)S(1)}, u32[]{:S(2)}, u32[]{:S(2)}) async-start(bf16[1024,4,128]{2,1,0:T(4,128)(2,1)} %copy.145), calls=%async_computation.8 | async-start | bytes 2097152 | tf_op jit(solution)/shard_map/all_to_all | solution.py:94
  278.3 1.3 copy.136
  279.6 2.6 copy.142
  282.2 1.3 copy.131
  283.5 9.9 %all-to-all-done.8 = bf16[1024,4,128]{2,1,0:T(4,128)(2,1)S(1)} async-done(((bf16[1024,4,128]{2,1,0:T(4,128)(2,1)}), bf16[1024,4,128]{2,1,0:T(4,128)(2,1)S(1)}, u32[]{:S(2)}, u32[]{:S(2)}) %all-to-all-start.8) | async-done | bytes 1048608 | tf_op jit(solution)/shard_map/all_to_all | solution.py:94
  293.4 1.3 copy.146
  (47 shorter events, 2.0 us)
Async XLA Ops:
  7.2 15.4 %copy-start.6 = (bf16[128,32,128]{2,1,0:T(8,128)(2,1)S(1)}, bf16[128,32,128]{2,1,0:T(8,128)(2,1)}, u32[]{:S(2)}) copy-start(bf16[128,32,128]{2,1,0:T(8,128)(2,1)} %param.7) | copy-start | bytes 3145732
  7.2 11.3 %all-to-all-start.2 = ((bf16[128,8,4]{0,2,1:T(4,128)(2,1)}), bf16[128,8,4]{0,2,1:T(4,128)(2,1)S(1)}, u32[]{:S(2)}, u32[]{:S(2)}) async-start(bf16[128,8,4]{0,2,1:T(4,128)(2,1)} %bitcast.154), calls=%async_computation.2 | async-start | bytes 16384 | tf_op jit(solution)/shard_map/all_to_all | solution.py:17
  18.4 19.3 %all-to-all-start.1 = ((bf16[128,32,128]{2,0,1:T(8,128)(2,1)}), bf16[128,32,128]{2,0,1:T(8,128)(2,1)S(1)}, u32[]{:S(2)}, u32[]{:S(2)}) async-start(bf16[128,32,128]{2,0,1:T(8,128)(2,1)} %copy.120), calls=%async_computation.1 | async-start | bytes 2097152 | tf_op jit(solution)/shard_map/all_to_all | solution.py:14
  37.7 19.5 %all-to-all-start.3 = ((bf16[128,32,128]{2,0,1:T(8,128)(2,1)}), bf16[128,32,128]{2,0,1:T(8,128)(2,1)S(1)}, u32[]{:S(2)}, u32[]{:S(2)}) async-start(bf16[128,32,128]{2,0,1:T(8,128)(2,1)} %copy.122), calls=%async_computation.3 | async-start | bytes 2097152 | tf_op jit(solution)/shard_map/all_to_all | solution.py:15
  42.0 119.5 %all-gather.6.cloned.1.call-start = ((), (), s32[]{:S(2)}) async-start(), calls=%async_computation.9 | async-start | bytes 4325376 | tf_op jit(solution)/shard_map/all_gather | solution.py:49
  43.9 123.5 %copy-start.8 = (f32[1024,4]{0,1:T(4,128)}, f32[1024,4]{0,1:T(4,128)S(1)}, u32[]{:S(2)}) copy-start(f32[1024,4]{0,1:T(4,128)S(1)} %get-tuple-element.7) | copy-start | bytes 49156
  44.0 18.8 %copy-start.1 = (bf16[128,8,4,128]{3,0,1,2:T(8,128)(2,1)}, bf16[128,8,4,128]{3,0,1,2:T(8,128)(2,1)S(1)}, u32[]{:S(2)}) copy-start(bf16[128,8,4,128]{3,0,1,2:T(8,128)(2,1)S(1)} %copy.121) | copy-start | bytes 3145732
  57.3 1.0 copy-start.4
  57.3 9.9 %copy-start.7 = (bf16[128,32,128]{2,1,0:T(8,128)(2,1)S(1)}, bf16[128,32,128]{2,1,0:T(8,128)(2,1)}, u32[]{:S(2)}) copy-start(bf16[128,32,128]{2,1,0:T(8,128)(2,1)} %param.8) | copy-start | bytes 3145732
  62.9 19.5 %all-to-all-start = ((bf16[128,32,128]{2,0,1:T(8,128)(2,1)}), bf16[128,32,128]{2,0,1:T(8,128)(2,1)S(1)}, u32[]{:S(2)}, u32[]{:S(2)}) async-start(bf16[128,32,128]{2,0,1:T(8,128)(2,1)} %copy.118), calls=%async_computation | async-start | bytes 2097152 | tf_op jit(solution)/shard_map/all_to_all | solution.py:13
  82.3 19.5 %all-to-all-start.5 = ((bf16[128,32,128]{2,0,1:T(8,128)(2,1)}), bf16[128,32,128]{2,0,1:T(8,128)(2,1)S(1)}, u32[]{:S(2)}, u32[]{:S(2)}) async-start(bf16[128,32,128]{2,0,1:T(8,128)(2,1)} %copy.132), calls=%async_computation.5 | async-start | bytes 2097152 | tf_op jit(solution)/shard_map/all_to_all | solution.py:16
  86.6 135.9 %all-gather.8.cloned.1.call-start = ((), (), s32[]{:S(2)}) async-start(), calls=%async_computation.10 | async-start | bytes 4325376 | tf_op jit(solution)/shard_map/all_gather | solution.py:55
  142.4 7.4 %copy-start.2 = (bf16[128,8,4,128]{3,0,1,2:T(8,128)(2,1)S(1)}, bf16[128,8,4,128]{3,0,1,2:T(8,128)(2,1)}, u32[]{:S(2)}) copy-start(bf16[128,8,4,128]{3,0,1,2:T(8,128)(2,1)} %copy-done.1) | copy-start | bytes 3145732
  149.8 4.0 %copy-start = (bf16[4,1024,1024]{2,1,0:T(8,128)(2,1)}, bf16[4,1024,1024]{2,1,0:T(8,128)(2,1)S(1)}, u32[]{:S(2)}) copy-start(bf16[4,1024,1024]{2,1,0:T(8,128)(2,1)S(1)} %multiply_convert_fusion) | copy-start | bytes 25165828
  161.6 5.9 %copy-start.5 = (f32[4,1024,128]{2,1,0:T(8,128)S(1)}, f32[4,1024,128]{2,1,0:T(8,128)}, u32[]{:S(2)}) copy-start(f32[4,1024,128]{2,1,0:T(8,128)} %fusion.14) | copy-start | bytes 6291460
  170.2 61.5 %all-to-all-start.6 = ((bf16[1024,4,128]{2,1,0:T(4,128)(2,1)}), bf16[1024,4,128]{2,1,0:T(4,128)(2,1)S(1)}, u32[]{:S(2)}, u32[]{:S(2)}) async-start(bf16[1024,4,128]{2,1,0:T(4,128)(2,1)} %copy.135), calls=%async_computation.6 | async-start | bytes 2097152 | tf_op jit(solution)/shard_map/all_to_all | solution.py:92
  231.8 22.8 %all-to-all-start.7 = ((bf16[1024,4,128]{2,1,0:T(4,128)(2,1)}), bf16[1024,4,128]{2,1,0:T(4,128)(2,1)}, u32[]{:S(2)}, u32[]{:S(2)}) async-start(bf16[1024,4,128]{2,1,0:T(4,128)(2,1)} %copy.141), calls=%async_computation.7 | async-start | bytes 2097152 | tf_op jit(solution)/shard_map/all_to_all | solution.py:93
  239.3 6.0 %copy-start.9 = (f32[1024,4]{0,1:T(4,128)S(1)}, f32[1024,4]{0,1:T(4,128)}, u32[]{:S(2)}) copy-start(f32[1024,4]{0,1:T(4,128)} %copy-done.8) | copy-start | bytes 49156
  254.5 19.5 %all-to-all-start.4 = ((bf16[1024,4,128]{2,1,0:T(4,128)(2,1)}), bf16[1024,4,128]{2,1,0:T(4,128)(2,1)S(1)}, u32[]{:S(2)}, u32[]{:S(2)}) async-start(bf16[1024,4,128]{2,1,0:T(4,128)(2,1)} %copy.130), calls=%async_computation.4 | async-start | bytes 2097152 | tf_op jit(solution)/shard_map/all_to_all | solution.py:91
  258.9 6.4 %copy-start.3 = (bf16[128,8,4,128]{3,0,1,2:T(8,128)(2,1)S(1)}, bf16[128,8,4,128]{3,0,1,2:T(8,128)(2,1)}, u32[]{:S(2)}) copy-start(bf16[128,8,4,128]{3,0,1,2:T(8,128)(2,1)} %copy-done.1) | copy-start | bytes 3145732
  274.0 19.4 %all-to-all-start.8 = ((bf16[1024,4,128]{2,1,0:T(4,128)(2,1)}), bf16[1024,4,128]{2,1,0:T(4,128)(2,1)S(1)}, u32[]{:S(2)}, u32[]{:S(2)}) async-start(bf16[1024,4,128]{2,1,0:T(4,128)(2,1)} %copy.145), calls=%async_computation.8 | async-start | bytes 2097152 | tf_op jit(solution)/shard_map/all_to_all | solution.py:94
Sparse Core Ops, SparseCore 0:
  60.4 79.9 all-gather.5
  143.5 78.9 all-gather.7
where the time goes:
time: 302 us
  waiting for transfers between devices  116 us (38%)
  matrix products  54.6 us (18%)
  starting transfers between devices  48.2 us (16%)
  blocking collectives  37.7 us (12%)
  local copies, waits for them, and re-layouts  24.7 us (8%)
  between operations  14.3 us (5%)
  other arithmetic  5.77 us (2%)
    all_gather x1, blocking collectives, shards(): totals = lax.all_gather(seg_total[None, :], 'seq', axis=0, tiled=True)  37.7 us
    all_gather x1, waiting for transfers between devices, shards(): lax.all_gather(local_qg[None], 'seq', axis=0, tiled=True).astype(f32)  36.4 us
    all_to_all x1, waiting for transfers between devices, shards(): lax.all_to_all(grad_out, 'head', split_axis=1, concat_axis=0, tiled=True)  15 us
    all_to_all x1, waiting for transfers between devices, shards(): lax.all_to_all(key_in, 'head', split_axis=1, concat_axis=0, tiled=True)  13.7 us
    all_to_all x1, waiting for transfers between devices, shards(): lax.all_to_all(query_in, 'head', split_axis=1, concat_axis=0, tiled=True)  13.7 us
    all_to_all x1, waiting for transfers between devices, shards(): lax.all_to_all(value_in, 'head', split_axis=1, concat_axis=0, tiled=True)  13.1 us
    all_to_all x1, waiting for transfers between devices, shards(): lax.all_to_all(grad_value, 'head', split_axis=0, concat_axis=1, tiled=True)  9.9 us
    unnamed x27, local copies, waits for them, and re-layouts  9.06 us
  transfers between devices with their start and end apart: 11, of which 9 were waited for; matrix products, arithmetic and copies ran while one was open for 27% of the time, Pallas kernels for 0%

commit v1 on v0

--- a/solution.py
+++ b/solution.py
@@ -4,6 +4,13 @@
 from jax.sharding import PartitionSpec as P
 
 precise = lax.Precision.HIGHEST
+
+
+def gather_over(array, name, dim):
+    count = lax.axis_size(name)
+    blocks = jnp.stack([array for _ in range(count)])
+    blocks = lax.all_to_all(blocks, name, split_axis=0, concat_axis=0)
+    return jnp.concatenate(blocks, axis=dim)
 
 
 def shards(query_in, key_in, value_in, grad_out, log_decay):
@@ -50,10 +57,7 @@
         precision=precise,
     )
     new_out = jnp.einsum(
-        "ih,ihde->hde",
-        w_out,
-        lax.all_gather(local_qg[None], "seq", axis=0, tiled=True).astype(f32),
-        precision=precise,
+        "ih,ihde->hde", w_out, gather_over(local_qg[None], "seq", 0).astype(f32), precision=precise
     )
     state_in = new_in
     state_out = new_out

time: 302 us -> 376 us (1.25)
  blocking collectives: 37.7 us -> 136 us
  waiting for transfers between devices: 116 us -> 74.4 us
  starting transfers between devices: 48.2 us -> 60.7 us
  local copies, waits for them, and re-layouts: 24.7 us -> 28.9 us
    all_gather x1, blocking collectives: 37.7 us -> 136 us  [shards(): totals = lax.all_gather(seg_total[None, :], 'seq', axis=0, tiled=True)]
    all_gather x1 -> x0, waiting for transfers between devices: 36.4 us -> none  [shards(): lax.all_gather(local_qg[None], 'seq', axis=0, tiled=True).astype(f32)]
    all_to_all x0 -> x1, starting transfers between devices: none -> 10.8 us  [gather_over(): blocks = lax.all_to_all(blocks, name, split_axis=0, concat_axis=0)]
    all_to_all x1, starting transfers between devices: 8.2 us -> 12 us  [shards(): lax.all_to_all(grad_query, 'head', split_axis=0, concat_axis=1, tiled=True)]
    unnamed x27 -> x31, local copies, waits for them, and re-layouts: 9.06 us -> 9.04 us
  transfers between devices with their start and end apart: 11 -> 11, of which waited for: 9 -> 8; matrix products, arithmetic and copies ran while one was open for 27% -> 23% of each run, Pallas kernels for 0% -> 0%
where the time goes in v1:
time: 376 us; the launch traced here: 375 us
  blocking collectives  136 us (36%)
  waiting for transfers between devices  74.4 us (20%)
  starting transfers between devices  60.7 us (16%)
  matrix products  53.6 us (14%)
  local copies, waits for them, and re-layouts  28.9 us (8%)
  between operations  14.3 us (4%)
  other arithmetic  6.74 us (2%)
    all_gather x1, blocking collectives, shards(): totals = lax.all_gather(seg_total[None, :], 'seq', axis=0, tiled=True)  136 us
    all_to_all x1, waiting for transfers between devices, shards(): lax.all_to_all(query_in, 'head', split_axis=1, concat_axis=0, tiled=True)  13.7 us
    all_to_all x1, waiting for transfers between devices, shards(): lax.all_to_all(key_in, 'head', split_axis=1, concat_axis=0, tiled=True)  13.7 us
    all_to_all x1, starting transfers between devices, shards(): lax.all_to_all(grad_query, 'head', split_axis=0, concat_axis=1, tiled=True)  12 us
    all_to_all x1, waiting for transfers between devices, shards(): lax.all_to_all(grad_out, 'head', split_axis=1, concat_axis=0, tiled=True)  11.7 us
    all_to_all x1, waiting for transfers between devices, shards(): lax.all_to_all(value_in, 'head', split_axis=1, concat_axis=0, tiled=True)  10.9 us
    all_to_all x1, starting transfers between devices, gather_over(): blocks = lax.all_to_all(blocks, name, split_axis=0, concat_axis=0)  10.8 us
    all_to_all x1, waiting for transfers between devices, shards(): lax.all_to_all(grad_value, 'head', split_axis=0, concat_axis=1, tiled=True)  9.9 us
  transfers between devices with their start and end apart: 11, of which 8 were waited for; matrix products, arithmetic and copies ran while one was open for 23% of the time, Pallas kernels for 0%

profile of v1, /device:TPU:1, one launch (start us, length us, event | category | flops | bytes accessed | tf_op | source)
XLA Modules:
  0.0 374.9 jit_solution(913253146165422030)
XLA Ops:
  7.2 6.6 %all-to-all-start.2 = ((bf16[128,8,4]{0,2,1:T(4,128)(2,1)}), bf16[128,8,4]{0,2,1:T(4,128)(2,1)S(1)}, u32[]{:S(2)}, u32[]{:S(2)}) async-start(bf16[128,8,4]{0,2,1:T(4,128)(2,1)} %bitcast.153), calls=%async_computation.2 | async-start | bytes 16384 | tf_op jit(solution)/shard_map/all_to_all | solution.py:24
  13.8 2.7 copy.118
  16.5 1.9 all-to-all-done.2
  18.4 4.2 %all-to-all-start = ((bf16[128,32,128]{2,0,1:T(8,128)(2,1)}), bf16[128,32,128]{2,0,1:T(8,128)(2,1)S(1)}, u32[]{:S(2)}, u32[]{:S(2)}) async-start(bf16[128,32,128]{2,0,1:T(8,128)(2,1)} %copy.118), calls=%async_computation | async-start | bytes 2097152 | tf_op jit(solution)/shard_map/all_to_all | solution.py:20
  22.6 1.4 copy.120
  24.0 13.7 %all-to-all-done = bf16[128,32,128]{2,0,1:T(8,128)(2,1)S(1)} async-done(((bf16[128,32,128]{2,0,1:T(8,128)(2,1)}), bf16[128,32,128]{2,0,1:T(8,128)(2,1)S(1)}, u32[]{:S(2)}, u32[]{:S(2)}) %all-to-all-start) | async-done | bytes 1048608 | tf_op jit(solution)/shard_map/all_to_all | solution.py:20
  37.7 4.3 %all-to-all-start.1 = ((bf16[128,32,128]{2,0,1:T(8,128)(2,1)}), bf16[128,32,128]{2,0,1:T(8,128)(2,1)S(1)}, u32[]{:S(2)}, u32[]{:S(2)}) async-start(bf16[128,32,128]{2,0,1:T(8,128)(2,1)} %copy.120), calls=%async_computation.1 | async-start | bytes 2097152 | tf_op jit(solution)/shard_map/all_to_all | solution.py:21
  42.0 1.4 copy.122
  43.4 13.7 %all-to-all-done.1 = bf16[128,32,128]{2,0,1:T(8,128)(2,1)S(1)} async-done(((bf16[128,32,128]{2,0,1:T(8,128)(2,1)}), bf16[128,32,128]{2,0,1:T(8,128)(2,1)S(1)}, u32[]{:S(2)}, u32[]{:S(2)}) %all-to-all-start.1) | async-done | bytes 1048608 | tf_op jit(solution)/shard_map/all_to_all | solution.py:21
  57.2 4.3 %all-to-all-start.3 = ((bf16[128,32,128]{2,0,1:T(8,128)(2,1)}), bf16[128,32,128]{2,0,1:T(8,128)(2,1)S(1)}, u32[]{:S(2)}, u32[]{:S(2)}) async-start(bf16[128,32,128]{2,0,1:T(8,128)(2,1)} %copy.122), calls=%async_computation.3 | async-start | bytes 2097152 | tf_op jit(solution)/shard_map/all_to_all | solution.py:22
  61.5 2.6 copy.132
  64.1 1.1 reduce-window.6
  65.7 10.9 %all-to-all-done.3 = bf16[128,32,128]{2,0,1:T(8,128)(2,1)S(1)} async-done(((bf16[128,32,128]{2,0,1:T(8,128)(2,1)}), bf16[128,32,128]{2,0,1:T(8,128)(2,1)S(1)}, u32[]{:S(2)}, u32[]{:S(2)}) %all-to-all-start.3) | async-done | bytes 1048608 | tf_op jit(solution)/shard_map/all_to_all | solution.py:22
  76.6 5.0 %all-to-all-start.5 = ((bf16[128,32,128]{2,0,1:T(8,128)(2,1)}), bf16[128,32,128]{2,0,1:T(8,128)(2,1)}, u32[]{:S(2)}, u32[]{:S(2)}) async-start(bf16[128,32,128]{2,0,1:T(8,128)(2,1)} %copy.132), calls=%async_computation.5 | async-start | bytes 2097152 | tf_op jit(solution)/shard_map/all_to_all | solution.py:23
  83.0 2.0 convolution_convert_fusion.1
  85.1 11.7 %all-to-all-done.5 = bf16[128,32,128]{2,0,1:T(8,128)(2,1)} async-done(((bf16[128,32,128]{2,0,1:T(8,128)(2,1)}), bf16[128,32,128]{2,0,1:T(8,128)(2,1)}, u32[]{:S(2)}, u32[]{:S(2)}) %all-to-all-start.5) | async-done | bytes 1048608 | tf_op jit(solution)/shard_map/all_to_all | solution.py:23
  96.8 1.3 copy.133
  98.1 1.3 convolution_convert_fusion
  99.4 3.0 stack.3
  102.5 10.8 %all-to-all-start.7 = ((bf16[32,1,4,128,128]{4,3,2,1,0:T(8,128)(2,1)}), bf16[32,1,4,128,128]{4,3,2,1,0:T(8,128)(2,1)}, u32[]{:S(2)}, u32[]{:S(2)}) async-start(bf16[32,1,4,128,128]{4,3,2,1,0:T(8,128)(2,1)} %stack.3), calls=%async_computation.7 | async-start | bytes 8388608 | tf_op jit(solution)/shard_map/all_to_all | solution.py:12
  113.3 1.3 iota_compare_fusion
  114.6 136.4 %all-gather.1 = f32[32,1,4]{2,1,0:T(1,128)S(1)} all-gather(f32[1,1,4]{2,1,0:T(1,128)S(1)} %bitcast.154), channel_id=1, replica_groups=mesh['seq'=32,'head'=8] {'seq'}, dimensions={0}, use_global_device_ids=true | all-gather | bytes 528 | tf_op jit(solution)/shard_map/all_gather | solution.py:43
  251.4 7.1 %multiply_convert_fusion = bf16[4,1024,1024]{2,1,0:T(8,128)(2,1)S(1)} fusion(bf16[1024,4,128]{2,0,1:T(8,128)(2,1)S(1)} %bitcast.119, bf16[1024,4,128]{2,0,1:T(8,128)(2,1)S(1)} %bitcast.140, f32[4,1024]{1,0:T(4,128)S(1)} %bitcast.149, pred[1024,1024]{1,0:T(8,128)(4,1)} %iota_compare_fusion), kind=kOutput, calls=%fused_computation | convolution fusion | flops 1098907648 | bytes 11550720 | tf_op jit(solution)/shard_map/the,she->hts/dot_general | solution.py:80
  258.5 4.0 %fusion.14 = f32[4,1024,128]{2,1,0:T(8,128)} fusion(bf16[4,1024,1024]{2,1,0:T(8,128)(2,1)S(1)} %multiply_convert_fusion, bf16[1024,4,128]{2,0,1:T(8,128)(2,1)S(1)} %bitcast.134), kind=kOutput, calls=%fused_computation.43 | convolution fusion | flops 1073741824 | bytes 11534336 | tf_op jit(solution)/shard_map/hts,shd->thd/dot_general | solution.py:83
  262.5 7.8 %multiply_convert_fusion.1 = bf16[4,1024,1024]{2,1,0:T(8,128)(2,1)} fusion(bf16[1024,4,128]{2,0,1:T(8,128)(2,1)S(1)} %bitcast.123, bf16[1024,4,128]{2,0,1:T(8,128)(2,1)S(1)} %bitcast.135, f32[4,1024]{1,0:T(4,128)S(1)} %bitcast.150, pred[1024,1024]{1,0:T(8,128)(4,1)S(1)} %copy-done.9), kind=kOutput, calls=%fused_computation.1 | convolution fusion | flops 1098907648 | bytes 11550720 | tf_op jit(solution)/shard_map/thd,shd->hts/dot_general | solution.py:73
  270.3 5.8 %fusion = f32[4,1,128,128]{3,1,2,0:T(1,128)S(1)} fusion(f32[32,4,1,1]{0,2,3,1:T(1,128)S(1)} %copy.148, bf16[32,4,128,128]{3,2,1,0:T(8,128)(2,1)} %bitcast.126), kind=kOutput, calls=%fused_computation.4 | convolution fusion | flops 25165824 | bytes 4456960 | tf_op jit(solution)/shard_map/ih,ihde->hde/dot_general | solution.py:53
  276.1 1.0 fusion.4
  277.1 1.8 copy.135
  278.9 12.0 %all-to-all-start.6 = ((bf16[1024,4,128]{2,1,0:T(4,128)(2,1)}), bf16[1024,4,128]{2,1,0:T(4,128)(2,1)S(1)}, u32[]{:S(2)}, u32[]{:S(2)}) async-start(bf16[1024,4,128]{2,1,0:T(4,128)(2,1)} %copy.135), calls=%async_computation.6 | async-start | bytes 2097152 | tf_op jit(solution)/shard_map/all_to_all | solution.py:96
  290.9 7.7 %fusion.15 = f32[4,1024,128]{2,1,0:T(8,128)} fusion(bf16[4,1024,1024]{2,1,0:T(8,128)(2,1)} %copy-done, bf16[1024,4,128]{2,0,1:T(8,128)(2,1)S(1)} %bitcast.124), kind=kOutput, calls=%fused_computation.44 | convolution fusion | flops 1073741824 | bytes 11534336 | tf_op jit(solution)/shard_map/hts,thd->shd/dot_general | solution.py:87
  298.6 3.7 multiply_reduce_fusion
  302.3 1.0 copy.162
  303.3 2.7 fusion.3
  306.0 1.8 copy.141
  307.8 4.8 %all-to-all-start.8 = ((bf16[1024,4,128]{2,1,0:T(4,128)(2,1)}), bf16[1024,4,128]{2,1,0:T(4,128)(2,1)}, u32[]{:S(2)}, u32[]{:S(2)}) async-start(bf16[1024,4,128]{2,1,0:T(4,128)(2,1)} %copy.141), calls=%async_computation.8 | async-start | bytes 2097152 | tf_op jit(solution)/shard_map/all_to_all | solution.py:97
  312.6 5.9 %fusion.13 = f32[4,1024,128]{2,1,0:T(8,128)S(1)} fusion(bf16[4,1024,1024]{2,1,0:T(8,128)(2,1)} %multiply_convert_fusion.1, bf16[1024,4,128]{2,0,1:T(8,128)(2,1)} %bitcast.139), kind=kOutput, calls=%fused_computation.42 | convolution fusion | flops 1073741824 | bytes 11534336 | tf_op jit(solution)/shard_map/hts,shd->thd/dot_general | solution.py:75
  319.6 1.8 copy.130
  321.4 6.5 %all-to-all-done.8 = bf16[1024,4,128]{2,1,0:T(4,128)(2,1)} async-done(((bf16[1024,4,128]{2,1,0:T(4,128)(2,1)}), bf16[1024,4,128]{2,1,0:T(4,128)(2,1)}, u32[]{:S(2)}, u32[]{:S(2)}) %all-to-all-start.8) | async-done | bytes 1048608 | tf_op jit(solution)/shard_map/all_to_all | solution.py:97
  327.8 4.3 %all-to-all-start.4 = ((bf16[1024,4,128]{2,1,0:T(4,128)(2,1)}), bf16[1024,4,128]{2,1,0:T(4,128)(2,1)S(1)}, u32[]{:S(2)}, u32[]{:S(2)}) async-start(bf16[1024,4,128]{2,1,0:T(4,128)(2,1)} %copy.130), calls=%async_computation.4 | async-start | bytes 2097152 | tf_op jit(solution)/shard_map/all_to_all | solution.py:95
  332.2 6.4 %fusion.16 = f32[4,1024,128]{2,1,0:T(8,128)S(1)} fusion(bf16[4,1024,1024]{2,1,0:T(8,128)(2,1)} %multiply_convert_fusion.1, bf16[1024,4,128]{2,0,1:T(8,128)(2,1)S(1)} %bitcast.121), kind=kOutput, calls=%fused_computation.45 | convolution fusion | flops 1073741824 | bytes 11534336 | tf_op jit(solution)/shard_map/hts,the->she/dot_general | solution.py:91
  339.6 1.8 copy.145
  341.4 5.9 %all-to-all-done.4 = bf16[1024,4,128]{2,1,0:T(4,128)(2,1)S(1)} async-done(((bf16[1024,4,128]{2,1,0:T(4,128)(2,1)}), bf16[1024,4,128]{2,1,0:T(4,128)(2,1)S(1)}, u32[]{:S(2)}, u32[]{:S(2)}) %all-to-all-start.4) | async-done | bytes 1048608 | tf_op jit(solution)/shard_map/all_to_all | solution.py:95
  347.3 4.3 %all-to-all-start.9 = ((bf16[1024,4,128]{2,1,0:T(4,128)(2,1)}), bf16[1024,4,128]{2,1,0:T(4,128)(2,1)S(1)}, u32[]{:S(2)}, u32[]{:S(2)}) async-start(bf16[1024,4,128]{2,1,0:T(4,128)(2,1)} %copy.145), calls=%async_computation.9 | async-start | bytes 2097152 | tf_op jit(solution)/shard_map/all_to_all | solution.py:98
  351.6 1.3 copy.136
  352.9 2.6 copy.142
  355.5 1.3 copy.131
  356.8 9.9 %all-to-all-done.9 = bf16[1024,4,128]{2,1,0:T(4,128)(2,1)S(1)} async-done(((bf16[1024,4,128]{2,1,0:T(4,128)(2,1)}), bf16[1024,4,128]{2,1,0:T(4,128)(2,1)S(1)}, u32[]{:S(2)}, u32[]{:S(2)}) %all-to-all-start.9) | async-done | bytes 1048608 | tf_op jit(solution)/shard_map/all_to_all | solution.py:98
  366.7 1.3 copy.146
  (51 shorter events, 4.4 us)
Async XLA Ops:
  7.2 15.4 %copy-start.7 = (bf16[128,32,128]{2,1,0:T(8,128)(2,1)S(1)}, bf16[128,32,128]{2,1,0:T(8,128)(2,1)}, u32[]{:S(2)}) copy-start(bf16[128,32,128]{2,1,0:T(8,128)(2,1)} %param.6) | copy-start | bytes 3145732
  7.2 11.3 %all-to-all-start.2 = ((bf16[128,8,4]{0,2,1:T(4,128)(2,1)}), bf16[128,8,4]{0,2,1:T(4,128)(2,1)S(1)}, u32[]{:S(2)}, u32[]{:S(2)}) async-start(bf16[128,8,4]{0,2,1:T(4,128)(2,1)} %bitcast.153), calls=%async_computation.2 | async-start | bytes 16384 | tf_op jit(solution)/shard_map/all_to_all | solution.py:24
  13.8 28.3 %copy-start.8 = (bf16[128,32,128]{2,1,0:T(8,128)(2,1)S(1)}, bf16[128,32,128]{2,1,0:T(8,128)(2,1)}, u32[]{:S(2)}) copy-start(bf16[128,32,128]{2,1,0:T(8,128)(2,1)} %param.7) | copy-start | bytes 3145732
  18.4 19.3 %all-to-all-start = ((bf16[128,32,128]{2,0,1:T(8,128)(2,1)}), bf16[128,32,128]{2,0,1:T(8,128)(2,1)S(1)}, u32[]{:S(2)}, u32[]{:S(2)}) async-start(bf16[128,32,128]{2,0,1:T(8,128)(2,1)} %copy.118), calls=%async_computation | async-start | bytes 2097152 | tf_op jit(solution)/shard_map/all_to_all | solution.py:20
  37.7 19.5 %all-to-all-start.1 = ((bf16[128,32,128]{2,0,1:T(8,128)(2,1)}), bf16[128,32,128]{2,0,1:T(8,128)(2,1)S(1)}, u32[]{:S(2)}, u32[]{:S(2)}) async-start(bf16[128,32,128]{2,0,1:T(8,128)(2,1)} %copy.120), calls=%async_computation.1 | async-start | bytes 2097152 | tf_op jit(solution)/shard_map/all_to_all | solution.py:21
  57.2 19.5 %all-to-all-start.3 = ((bf16[128,32,128]{2,0,1:T(8,128)(2,1)}), bf16[128,32,128]{2,0,1:T(8,128)(2,1)S(1)}, u32[]{:S(2)}, u32[]{:S(2)}) async-start(bf16[128,32,128]{2,0,1:T(8,128)(2,1)} %copy.122), calls=%async_computation.3 | async-start | bytes 2097152 | tf_op jit(solution)/shard_map/all_to_all | solution.py:22
  76.6 20.2 %all-to-all-start.5 = ((bf16[128,32,128]{2,0,1:T(8,128)(2,1)}), bf16[128,32,128]{2,0,1:T(8,128)(2,1)}, u32[]{:S(2)}, u32[]{:S(2)}) async-start(bf16[128,32,128]{2,0,1:T(8,128)(2,1)} %copy.132), calls=%async_computation.5 | async-start | bytes 2097152 | tf_op jit(solution)/shard_map/all_to_all | solution.py:23
  81.6 188.7 %all-gather.4.cloned.1.call-start = ((), (), s32[]{:S(2)}) async-start(), calls=%async_computation.10 | async-start | bytes 4325376 | tf_op jit(solution)/shard_map/all_gather | solution.py:56
  81.9 194.2 %copy-start.10 = (f32[1024,4]{0,1:T(4,128)}, f32[1024,4]{0,1:T(4,128)S(1)}, u32[]{:S(2)}) copy-start(f32[1024,4]{0,1:T(4,128)S(1)} %get-tuple-element.7) | copy-start | bytes 49156
  82.0 1.0 copy-start.1
  82.1 2.9 copy-start.4
  102.5 148.9 %copy-start.5 = (bf16[128,8,4,128]{3,0,1,2:T(8,128)(2,1)S(1)}, bf16[128,8,4,128]{3,0,1,2:T(8,128)(2,1)}, u32[]{:S(2)}) copy-start(bf16[128,8,4,128]{3,0,1,2:T(8,128)(2,1)} %copy-done.4) | copy-start | bytes 3145732
  102.5 176.4 %all-to-all-start.7 = ((bf16[32,1,4,128,128]{4,3,2,1,0:T(8,128)(2,1)}), bf16[32,1,4,128,128]{4,3,2,1,0:T(8,128)(2,1)}, u32[]{:S(2)}, u32[]{:S(2)}) async-start(bf16[32,1,4,128,128]{4,3,2,1,0:T(8,128)(2,1)} %stack.3), calls=%async_computation.7 | async-start | bytes 8388608 | tf_op jit(solution)/shard_map/all_to_all | solution.py:12
  251.4 7.1 %copy-start.2 = (bf16[128,8,4,128]{3,0,1,2:T(8,128)(2,1)S(1)}, bf16[128,8,4,128]{3,0,1,2:T(8,128)(2,1)}, u32[]{:S(2)}) copy-start(bf16[128,8,4,128]{3,0,1,2:T(8,128)(2,1)} %copy-done.1) | copy-start | bytes 3145732
  258.5 4.0 %copy-start = (bf16[4,1024,1024]{2,1,0:T(8,128)(2,1)}, bf16[4,1024,1024]{2,1,0:T(8,128)(2,1)S(1)}, u32[]{:S(2)}) copy-start(bf16[4,1024,1024]{2,1,0:T(8,128)(2,1)S(1)} %multiply_convert_fusion) | copy-start | bytes 25165828
  258.5 4.0 %copy-start.9 = (pred[1024,1024]{1,0:T(8,128)(4,1)S(1)}, pred[1024,1024]{1,0:T(8,128)(4,1)}, u32[]{:S(2)}) copy-start(pred[1024,1024]{1,0:T(8,128)(4,1)} %iota_compare_fusion) | copy-start | bytes 3145732
  270.3 5.9 %copy-start.6 = (f32[4,1024,128]{2,1,0:T(8,128)S(1)}, f32[4,1024,128]{2,1,0:T(8,128)}, u32[]{:S(2)}) copy-start(f32[4,1024,128]{2,1,0:T(8,128)} %fusion.14) | copy-start | bytes 6291460
  278.9 28.9 %all-to-all-start.6 = ((bf16[1024,4,128]{2,1,0:T(4,128)(2,1)}), bf16[1024,4,128]{2,1,0:T(4,128)(2,1)S(1)}, u32[]{:S(2)}, u32[]{:S(2)}) async-start(bf16[1024,4,128]{2,1,0:T(4,128)(2,1)} %copy.135), calls=%async_computation.6 | async-start | bytes 2097152 | tf_op jit(solution)/shard_map/all_to_all | solution.py:96
  307.8 20.0 %all-to-all-start.8 = ((bf16[1024,4,128]{2,1,0:T(4,128)(2,1)}), bf16[1024,4,128]{2,1,0:T(4,128)(2,1)}, u32[]{:S(2)}, u32[]{:S(2)}) async-start(bf16[1024,4,128]{2,1,0:T(4,128)(2,1)} %copy.141), calls=%async_computation.8 | async-start | bytes 2097152 | tf_op jit(solution)/shard_map/all_to_all | solution.py:97
  312.6 6.0 %copy-start.11 = (f32[1024,4]{0,1:T(4,128)S(1)}, f32[1024,4]{0,1:T(4,128)}, u32[]{:S(2)}) copy-start(f32[1024,4]{0,1:T(4,128)} %copy-done.10) | copy-start | bytes 49156
  327.8 19.5 %all-to-all-start.4 = ((bf16[1024,4,128]{2,1,0:T(4,128)(2,1)}), bf16[1024,4,128]{2,1,0:T(4,128)(2,1)S(1)}, u32[]{:S(2)}, u32[]{:S(2)}) async-start(bf16[1024,4,128]{2,1,0:T(4,128)(2,1)} %copy.130), calls=%async_computation.4 | async-start | bytes 2097152 | tf_op jit(solution)/shard_map/all_to_all | solution.py:95
  332.2 6.4 %copy-start.3 = (bf16[128,8,4,128]{3,0,1,2:T(8,128)(2,1)S(1)}, bf16[128,8,4,128]{3,0,1,2:T(8,128)(2,1)}, u32[]{:S(2)}) copy-start(bf16[128,8,4,128]{3,0,1,2:T(8,128)(2,1)} %copy-done.1) | copy-start | bytes 3145732
  347.3 19.5 %all-to-all-start.9 = ((bf16[1024,4,128]{2,1,0:T(4,128)(2,1)}), bf16[1024,4,128]{2,1,0:T(4,128)(2,1)S(1)}, u32[]{:S(2)}, u32[]{:S(2)}) async-start(bf16[1024,4,128]{2,1,0:T(4,128)(2,1)} %copy.145), calls=%async_computation.9 | async-start | bytes 2097152 | tf_op jit(solution)/shard_map/all_to_all | solution.py:98
Sparse Core Ops, SparseCore 0:
  85.6 136.5 all-gather.3
